TPU v7x, 32 devices: a whole 2x2x4 slice. The times are simulated.
32 devices in a mesh: parts: 2 (over x), view: 8 (over z, y), slab: 2 (over core).
Axes of the slice: x: 2, y: 2, z: 4, core: 2. Of those that a mesh axis runs over, the one named last changes fastest.
Arguments:
- activity: bfloat16 [128, 32, 256], P(('parts', 'view'), 'slab'), parts along dimension 0, may hold values from 0.6 to 11.2
- histo_counts: int32 [32, 64, 32, 256], P(('parts', 'view'), None, 'slab'), parts along dimension 0, may hold values from 0 to 22
- background: bfloat16 [32, 32, 256], P(('parts', 'view'), 'slab'), parts along dimension 0, may hold values from 0.5 to 2
- blur_values: bfloat16 [16, 3, 256, 32], P('view'), may hold values from 0.0041503906 to 0.020751953
- band_start: int32 [16, 3, 256], P('view'), may hold values from 0 to 224, as said below
Outputs:
- gradient: float32 [128, 32, 256], P(('parts', 'view'), 'slab'), parts along dimension 0
There are 2 independent parts, one for each index of `parts`. A program takes and returns all parts, laid end to end along the dimension named above; an argument that names none is the same for every part. Nothing has to cross between parts.
Inputs may be any that keep to these rules, and one draw needn't show every extreme that they name: Each band lies inside the matrix: columns band_start to band_start + 31.
All inputs are finite; a program needn't handle non-finite values.
Results may differ from a plain program's by a relative error of at most 0.0003.
Values may be sent and summed in bfloat16 or wider, within the bound.
A program may use at most 64 MiB of HBM per device.

v0:
```python
import functools

import jax
import jax.numpy as jnp
from jax import lax
from jax.experimental import pallas as pl
from jax.experimental.pallas import tpu as pltpu
from jax.sharding import PartitionSpec as P

MESH = pl.DeviceIdType.MESH
PAIR = 2
SLABS = 2


CODE_MAX = 32767.0
TINY = 1e-30
VMEM_LIMIT = 63 << 20


def encode(block):
    top = jnp.max(jnp.abs(block), axis=(0, 1), keepdims=False)[None, :]
    scale = jnp.where(top > TINY, CODE_MAX / jnp.maximum(top, TINY), 0.0)
    code = jnp.round(block * scale[None]).astype(jnp.int32).astype(jnp.int16)
    return code, jnp.broadcast_to(top * (1.0 / CODE_MAX), (8, block.shape[2]))


def decode(code, unit):
    return code.astype(jnp.int32).astype(jnp.float32) * unit[None, 0:1, :]


def kernel(
    groups, act_hbm, counts_ref, back_hbm, values_hbm, starts_hbm, out_ref,
    act_ref, back_ref, values_ref, starts_ref,
    acts, edges, edge_own, counts, forward_w, backward_w, kept, part_code, part_unit, pair_code, pair_unit, sum_code, sum_unit, owner_code, owner_unit, halo_out, halo_in,
    load_sem, counts_sem, line_send, line_recv, pair_send, pair_recv, edge_send, edge_recv,
    halo_send, halo_recv, part_send, part_recv, sum_send, sum_recv, part_unit_send, part_unit_recv, sum_unit_send, sum_unit_recv,
):
    part = lax.axis_index("parts")
    view = lax.axis_index("view")
    slab = lax.axis_index("slab")
    members = groups * PAIR
    last = groups - 1
    hi = view // PAIR
    lo = view % PAIR
    other = 1 - lo
    rows, slices, width = act_ref.shape
    views = back_ref.shape[0]
    taps = values_ref.shape[0] // views
    group_rows = PAIR * rows

    def at(hi_index, lo_index, slab_index):
        return (part, hi_index * PAIR + lo_index, slab_index)

    def met(step):
        key = (groups - step) % groups
        index, unit = 0, 1
        while unit < groups:
            index += ((hi // unit + key // unit) % 2) * unit
            unit *= 2
        return index

    barrier = pltpu.get_barrier_semaphore()
    for step in range(members):
        pl.semaphore_signal(
            barrier, inc=1, device_id=(part, lax.rem(view + step, members), 1 - slab), device_id_type=MESH
        )
    for step in range(1, groups):
        pl.semaphore_signal(barrier, inc=1, device_id=at(met(step), lo, slab), device_id_type=MESH)
    pl.semaphore_signal(barrier, inc=1, device_id=at(hi, other, slab), device_id_type=MESH)
    pl.semaphore_signal(barrier, inc=1, device_id=at(met(last), other, slab), device_id_type=MESH)

    def counts_copy(step):
        first = pl.multiple_of(met(step) * group_rows, group_rows)
        return pltpu.make_async_copy(
            counts_ref.at[:, pl.ds(first, group_rows)], counts.at[step], counts_sem.at[step]
        )

    loads = [
        pltpu.make_async_copy(source, target, load_sem.at[index])
        for index, (source, target) in enumerate(
            ((values_hbm, values_ref), (starts_hbm, starts_ref), (act_hbm, act_ref), (back_hbm, back_ref))
        )
    ]
    for load in loads:
        load.start()
    for step in range(groups):
        counts_copy(step).start()
    for load in loads:
        load.wait()
    own = act_ref[...]
    own_wide = own.astype(jnp.float32)
    edge_own[...] = jnp.where(slab == 0, own_wide[:, slices - 1, :], own_wide[:, 0, :]).astype(jnp.bfloat16)
    acts[view] = own

    def build(which):
        view_index, tap = which // taps, which % taps
        start = starts_ref[tap, view_index : view_index + 1, :]
        turned = jnp.concatenate(
            [values_ref[which].astype(jnp.float32), jnp.zeros((8, width), jnp.float32)], axis=0
        )
        shift = 1
        while shift < 8:
            turned = jnp.where((start & shift) != 0, pltpu.roll(turned, shift, axis=0), turned)
            shift *= 2
        while shift < width:
            extra = min(shift, width - turned.shape[0])
            plain = jnp.concatenate([turned, jnp.zeros((extra, width), jnp.float32)], axis=0)
            moved = jnp.concatenate([jnp.zeros((shift, width), jnp.float32), turned], axis=0)[: plain.shape[0]]
            turned = jnp.where((start & shift) != 0, moved, plain)
            shift *= 2
        forward_w[tap * width : (tap + 1) * width, view_index * width : (view_index + 1) * width] = (
            turned.astype(jnp.bfloat16)
        )
        backward_w[view_index * width : (view_index + 1) * width, tap * width : (tap + 1) * width] = (
            turned.T.astype(jnp.bfloat16)
        )

    total = views * taps
    for which in range(total):
        build(which)

    pl.semaphore_wait(barrier, members + groups + 1)

    def pair_copy(step, source):
        return pltpu.make_async_remote_copy(
            src_ref=source, dst_ref=acts.at[met(step) * PAIR + lo],
            send_sem=pair_send.at[step], recv_sem=pair_recv.at[step],
            device_id=at(hi, other, slab), device_id_type=MESH,
        )

    def near_copy():
        return pltpu.make_async_remote_copy(
            src_ref=acts.at[hi * PAIR + other], dst_ref=acts.at[hi * PAIR + other],
            send_sem=pair_send.at[last], recv_sem=pair_recv.at[last],
            device_id=at(met(last), lo, slab), device_id_type=MESH,
        )

    def line_copy(step):
        return pltpu.make_async_remote_copy(
            src_ref=act_ref, dst_ref=acts.at[view],
            send_sem=line_send.at[step], recv_sem=line_recv.at[step],
            device_id=at(met(step), lo, slab), device_id_type=MESH,
        )

    def edge_copy(step):
        return pltpu.make_async_remote_copy(
            src_ref=edge_own, dst_ref=edges.at[view],
            send_sem=edge_send.at[step], recv_sem=edge_recv.at[step],
            device_id=at(met(step // PAIR), (lo + step % PAIR) % PAIR, 1 - slab), device_id_type=MESH,
        )

    pair_copy(0, act_ref).start()
    for step in range(1, groups):
        line_copy(step).start()
    for step in range(members):
        edge_copy(step).start()

    slice_at = lax.broadcasted_iota(jnp.int32, (group_rows, slices, width), 1)
    inner = jnp.where(slab == 0, slices - 1, 0)

    def halo_copies(step):
        return [
            pltpu.make_async_remote_copy(
                src_ref=halo_out.at[step, keeper], dst_ref=halo_in.at[step, index],
                send_sem=halo_send.at[step, index], recv_sem=halo_recv.at[step, index],
                device_id=at(hi, keeper, 1 - slab), device_id_type=MESH,
            )
            for index, keeper in enumerate((lo, other))
        ]

    def part_copies(step, target):
        return [
            pltpu.make_async_remote_copy(
                src_ref=source.at[step], dst_ref=landing.at[step],
                send_sem=send.at[step], recv_sem=recv.at[step],
                device_id=at(target, other, slab), device_id_type=MESH,
            )
            for source, landing, send, recv in (
                (part_unit, pair_unit, part_unit_send, part_unit_recv),
                (part_code, pair_code, part_send, part_recv),
            )
        ]

    def sum_copies(step):
        return [
            pltpu.make_async_remote_copy(
                src_ref=source.at[step], dst_ref=target.at[step],
                send_sem=send.at[step], recv_sem=recv.at[step],
                device_id=at(met(step), lo, slab), device_id_type=MESH,
            )
            for source, target, send, recv in (
                (sum_unit, owner_unit, sum_unit_send, sum_unit_recv),
                (sum_code, owner_code, sum_send, sum_recv),
            )
        ]

    def relay(step):
        line_copy(step).wait_recv()
        pair_copy(step, acts.at[met(step) * PAIR + lo]).start()

    def kept_sum(step):
        for copy in halo_copies(step):
            copy.wait_recv()
        halo = (halo_in[step, 0] + halo_in[step, 1]).reshape(rows, 1, width)
        return kept[step] + jnp.where(slice_at[:rows] == inner, halo, 0.0)

    def pair_part(step):
        for copy in part_copies(step, hi):
            copy.wait_recv()
        return decode(pair_code[step], pair_unit[step])

    def pass_on(step, value):
        sum_code[step], sum_unit[step] = encode(value)
        for copy in sum_copies(step):
            copy.start()

    def one_group(step, carry):
        group = met(step)
        for which in range(PAIR):
            edge_copy(step * PAIR + which).wait_recv()
        pair_copy(step, act_ref).wait_recv()

        @pl.when(step == 0)
        def _():
            near_copy().start()

        @pl.when(step == last)
        def _():
            line_copy(last).wait_recv()

        image = acts[pl.ds(group * PAIR, PAIR)].astype(jnp.float32).reshape(group_rows, slices, width)
        edge = edges[pl.ds(group * PAIR, PAIR)].astype(jnp.float32).reshape(group_rows, 1, width)
        lower = jnp.where(slice_at == 0, jnp.where(slab == 0, 0.0, edge), pltpu.roll(image, 1, axis=1))
        upper = jnp.where(
            slice_at == slices - 1, jnp.where(slab == 0, edge, 0.0), pltpu.roll(image, slices - 1, axis=1)
        )
        stacked = jnp.concatenate(
            [x.reshape(-1, width).astype(jnp.bfloat16) for x in (lower, image, upper)], axis=1
        )
        summed = jnp.dot(stacked, forward_w[...], preferred_element_type=jnp.float32)
        counts_copy(step).wait()
        ratios = []
        ratio_edges = []
        for view_index in range(views):
            expected = (
                summed[:, view_index * width : (view_index + 1) * width].reshape(group_rows, slices, width)
                + back_ref[view_index].astype(jnp.float32)[None]
            )
            ratio = counts[step, view_index].astype(jnp.float32) / expected - 1.0
            ratio_edges.append(
                jnp.where(slab == 0, ratio[:, slices - 1, :], ratio[:, 0, :]).astype(jnp.bfloat16)
            )
            ratios.append(ratio.reshape(-1, width).astype(jnp.bfloat16))
        outer = pl.multiple_of((1 - slab) * ((taps - 1) * width), width)
        halo_out[step] = jnp.dot(
            jnp.concatenate(ratio_edges, axis=1), backward_w[:, pl.ds(outer, width)],
            preferred_element_type=jnp.float32,
        ).reshape(PAIR, rows, width)
        for copy in halo_copies(step):
            copy.start()
        spread = jnp.dot(
            jnp.concatenate(ratios, axis=1), backward_w[...], preferred_element_type=jnp.float32
        ).reshape(group_rows, slices, taps * width)
        from_upper = pltpu.roll(spread[:, :, :width], slices - 1, axis=1)
        from_lower = pltpu.roll(spread[:, :, 2 * width :], 1, axis=1)
        from_upper = jnp.where(slice_at == slices - 1, 0.0, from_upper)
        from_lower = jnp.where(slice_at == 0, 0.0, from_lower)
        spread_sum = (spread[:, :, width : 2 * width] + from_upper + from_lower).reshape(
            PAIR, rows, slices, width
        )
        kept[step] = jnp.where(lo == 0, spread_sum[0], spread_sum[1])
        part_code[step], part_unit[step] = encode(jnp.where(lo == 0, spread_sum[1], spread_sum[0]))

        @pl.when(step == 0)
        def _():
            for later in range(1, last):
                relay(later)

        @pl.when(step < last)
        def _():
            for copy in part_copies(step, hi):
                copy.start()

        @pl.when(step == last)
        def _():
            for copy in part_copies(step, met(last)):
                copy.start()

        @pl.when(step > 1)
        def _():
            pass_on(step - 1, kept_sum(step - 1) + pair_part(step - 1))

        return carry

    lax.fori_loop(0, groups, one_group, 0)
    pass_on(last, kept_sum(last))
    gradient = kept_sum(0) + pair_part(0)
    for step in range(1, groups):
        for copy in sum_copies(step):
            copy.wait_recv()
        gradient = gradient + decode(owner_code[step], owner_unit[step])
    out_ref[...] = gradient + pair_part(last)

    for step in range(1, groups):
        line_copy(step).wait_send()
        for copy in sum_copies(step):
            copy.wait_send()
    for step in range(groups):
        pair_copy(step, act_ref).wait_send()
        for copy in halo_copies(step):
            copy.wait_send()
        for copy in part_copies(step, hi):
            copy.wait_send()
    for step in range(members):
        edge_copy(step).wait_send()


def per_device(activity, histo_counts, background, blur_values, band_start):
    members = lax.axis_size("view")
    groups = members // PAIR
    rows, slices, width = activity.shape
    views, taps, _, band = blur_values.shape
    group_rows = PAIR * rows
    dma = pltpu.SemaphoreType.DMA
    block = (rows, slices, width)
    vmem = pl.BlockSpec(memory_space=pltpu.VMEM)
    return pl.pallas_call(
        functools.partial(kernel, groups),
        out_shape=jax.ShapeDtypeStruct(block, jnp.float32),
        in_specs=[pl.BlockSpec(memory_space=pl.ANY)] * 5,
        out_specs=vmem,
        scratch_shapes=[
            pltpu.VMEM(block, jnp.bfloat16),
            pltpu.VMEM(background.shape, jnp.bfloat16),
            pltpu.VMEM((views * taps, band, width), jnp.bfloat16),
            pltpu.VMEM((taps, views, width), jnp.int32),
            pltpu.VMEM((members,) + block, jnp.bfloat16),
            pltpu.VMEM((members, rows, width), jnp.bfloat16),
            pltpu.VMEM((rows, width), jnp.bfloat16),
            pltpu.VMEM((groups, views, group_rows, slices, width), jnp.int32),
            pltpu.VMEM((taps * width, views * width), jnp.bfloat16),
            pltpu.VMEM((views * width, taps * width), jnp.bfloat16),
            pltpu.VMEM((groups,) + block, jnp.float32),
            pltpu.VMEM((groups,) + block, jnp.int16),
            pltpu.VMEM((groups, 8, width), jnp.float32),
            pltpu.VMEM((groups,) + block, jnp.int16),
            pltpu.VMEM((groups, 8, width), jnp.float32),
            pltpu.VMEM((groups,) + block, jnp.int16),
            pltpu.VMEM((groups, 8, width), jnp.float32),
            pltpu.VMEM((groups,) + block, jnp.int16),
            pltpu.VMEM((groups, 8, width), jnp.float32),
            pltpu.VMEM((groups, PAIR, rows, width), jnp.float32),
            pltpu.VMEM((groups, PAIR, rows, width), jnp.float32),
            dma((4,)),
            dma((groups,)),
            dma((groups,)), dma((groups,)),
            dma((groups,)), dma((groups,)),
            dma((members,)), dma((members,)),
            dma((groups, PAIR)), dma((groups, PAIR)),
            dma((groups,)), dma((groups,)),
            dma((groups,)), dma((groups,)),
            dma((groups,)), dma((groups,)),
            dma((groups,)), dma((groups,)),
        ],
        compiler_params=pltpu.CompilerParams(collective_id=0, has_side_effects=True, vmem_limit_bytes=VMEM_LIMIT),
        name="poisson_gradient",
    )(
        activity, histo_counts, background,
        jnp.swapaxes(blur_values, 2, 3).reshape(views * taps, band, width), jnp.swapaxes(band_start, 0, 1),
    )


def solution(mesh):
    placed = (
        P(("parts", "view"), "slab", None),
        P(("parts", "view"), None, "slab", None),
        P(("parts", "view"), "slab", None),
        P("view", None, None, None),
        P("view", None, None),
    )
    return jax.shard_map(
        per_device,
        mesh=mesh,
        in_specs=placed,
        out_specs=P(("parts", "view"), "slab", None),
        check_vma=False,
    )
```

profile of v0, /device:TPU:0, one launch (start us, length us, event | category | flops | bytes accessed | tf_op | source)
XLA Modules:
  0.0 31.2 jit_solution(182040992243110451)
XLA Ops:
  0.0 29.6 %poisson_gradient.1 = f32[8,16,256]{2,1,0:T(8,128)} custom-call(bf16[8,16,256]{2,1,0:T(8,128)(2,1)} %act_hbm.1, s32[2,64,16,256]{3,2,1,0:T(8,128)} %counts_ref.1, bf16[2,16,256]{2,1,0:T(8,128)(2,1)} %back_hbm.1, bf16[6,32,256]{2,1,0:T(8,128)(2,1)} %bitcast.4, s32[3,2,256]{2,1,0:T(2,128)} %bitcast.5), custom_call_target="tpu_custom_call" | custom-call | tf_op jit(solution)/shard_map/poisson_gradient/pallas_call | solution.py:327
  29.6 1.6 %copy.7 = f32[8,16,256]{2,1,0:T(8,128)} copy(f32[8,16,256]{2,1,0:T(8,128)} %poisson_gradient.1) | data formatting | bytes 262144
where the time goes:
time: 31.3 us; the launch traced here: 31.2 us
  Pallas kernels  29.6 us (95%)
  local copies, waits for them, and re-layouts  1.57 us (5%)
    pallas_call x1, Pallas kernels, per_device(): pl.pallas_call(functools.partial(kernel, groups), out_shape=jax.ShapeDtyp...  29.6 us
    unnamed x1, local copies, waits for them, and re-layouts  1.57 us

commit v1 on v0

v1 whole, which is shorter than its diff:
```python
import functools

import jax
import jax.numpy as jnp
from jax import lax
from jax.experimental import pallas as pl
from jax.experimental.pallas import tpu as pltpu
from jax.sharding import PartitionSpec as P

MESH = pl.DeviceIdType.MESH
PAIR = 2


CODE_MAX = 32767.0
TINY = 1e-30
VMEM_LIMIT = 63 << 20


def encode(block):
    top = jnp.max(jnp.abs(block), axis=(0, 1), keepdims=False)[None, :]
    scale = jnp.where(top > TINY, CODE_MAX / jnp.maximum(top, TINY), 0.0)
    code = jnp.round(block * scale[None]).astype(jnp.int32).astype(jnp.int16)
    return code, top * (1.0 / CODE_MAX)


def decode(code, unit):
    return code.astype(jnp.int32).astype(jnp.float32) * unit[None]


def kernel(
    groups, rows, act_hbm, counts_hbm, back_hbm, values_hbm, starts_hbm, out_ref,
    back_ref, values_ref, starts_ref,
    acts, edge_own, counts, forward_w, backward_w, whole, kept, part_code, part_unit, pair_code, pair_unit,
    sum_code, sum_unit, owner_code, owner_unit, halo_out, halo_in,
    load_sem, counts_sem, ready, pair_ready, line_send, line_recv, line_edge_send, line_edge_recv,
    pair_send, pair_recv, pair_edge_send, pair_edge_recv, edge_send, edge_recv, halo_send, halo_recv,
    part_send, part_recv, part_unit_send, part_unit_recv, sum_send, sum_recv, sum_unit_send, sum_unit_recv,
):
    part = lax.axis_index("parts")
    view = lax.axis_index("view")
    slab = lax.axis_index("slab")
    last = groups - 1
    hi = view // PAIR
    lo = view % PAIR
    other = 1 - lo
    area, width = act_hbm.shape
    slices = area // rows
    views = back_ref.shape[0]
    taps = values_ref.shape[0] // views
    group_rows = PAIR * rows

    def at(hi_index, lo_index, slab_index):
        return (part, hi_index * PAIR + lo_index, slab_index)

    def near(step):
        both = jnp.minimum(hi, last - hi)
        reach = (step + 1) // 2
        around = jnp.where(step % 2 == 1, hi - reach, hi + reach)
        beyond = jnp.where(hi < last - hi, step, last - step)
        return jnp.where(step <= 2 * both, around, beyond)

    barrier = pltpu.get_barrier_semaphore()
    pl.semaphore_signal(barrier, inc=1, device_id=at(hi, lo, 1 - slab), device_id_type=MESH)

    @pl.when(lo == 0)
    def _():
        pl.semaphore_signal(barrier, inc=1, device_id=at(hi, 1, slab), device_id_type=MESH)

    for index in range(1, groups):

        @pl.when(index > hi)
        def _():
            pl.semaphore_signal(barrier, inc=1, device_id=at(index, lo, slab), device_id_type=MESH)

    def counts_copy(step):
        first = pl.multiple_of(near(step) * group_rows, group_rows)
        return pltpu.make_async_copy(
            counts_hbm.at[:, pl.ds(first, group_rows)], counts.at[step], counts_sem.at[step]
        )

    def block_of(index):
        return acts.at[index, pl.ds(0, area)]

    def edge_of(index):
        return acts.at[index, pl.ds(area, rows)]

    loads = [
        pltpu.make_async_copy(source, target, load_sem.at[index])
        for index, (source, target) in enumerate(
            (
                (act_hbm, block_of(view)), (values_hbm, values_ref), (starts_hbm, starts_ref),
                (back_hbm, back_ref),
            )
        )
    ]
    for load in loads:
        load.start()
    for step in range(groups):
        counts_copy(step).start()
    loads[0].wait()
    own = acts[view, :area].astype(jnp.float32).reshape(rows, slices, width)
    edge_own[...] = jnp.where(slab == 0, own[:, slices - 1, :], own[:, 0, :]).astype(jnp.bfloat16)

    def line_copy(index):
        return pltpu.make_async_remote_copy(
            src_ref=act_hbm, dst_ref=block_of(view),
            send_sem=line_send.at[index], recv_sem=line_recv.at[hi],
            device_id=at(index, lo, slab), device_id_type=MESH,
        )

    def line_edge_copy(index):
        return pltpu.make_async_remote_copy(
            src_ref=edge_of(view), dst_ref=edge_of(view),
            send_sem=line_edge_send.at[index], recv_sem=line_edge_recv.at[hi],
            device_id=at(index, lo, slab), device_id_type=MESH,
        )

    def line_wait(index):
        source = index * PAIR + lo
        for target, recv in ((block_of(source), line_recv), (edge_of(source), line_edge_recv)):
            pltpu.make_async_remote_copy(
                src_ref=target, dst_ref=target,
                send_sem=line_send.at[index], recv_sem=recv.at[index],
                device_id=at(hi, other, slab), device_id_type=MESH,
            ).wait_recv()

    def pair_copy(index, source):
        return pltpu.make_async_remote_copy(
            src_ref=source, dst_ref=block_of(index * PAIR + lo),
            send_sem=pair_send.at[index], recv_sem=pair_recv.at[index],
            device_id=at(hi, other, slab), device_id_type=MESH,
        )

    def pair_edge_copy(index):
        return pltpu.make_async_remote_copy(
            src_ref=edge_of(index * PAIR + lo), dst_ref=edge_of(index * PAIR + lo),
            send_sem=pair_edge_send.at[index], recv_sem=pair_edge_recv.at[index],
            device_id=at(hi, other, slab), device_id_type=MESH,
        )

    edge_copy = pltpu.make_async_remote_copy(
        src_ref=edge_own, dst_ref=edge_of(view), send_sem=edge_send, recv_sem=edge_recv,
        device_id=at(hi, lo, 1 - slab), device_id_type=MESH,
    )

    pl.semaphore_wait(barrier, 1 + hi + lo)

    @pl.when(lo == 1)
    def _():
        pl.semaphore_signal(pair_ready, inc=1, device_id=at(hi, 0, slab), device_id_type=MESH)

    for index in range(last):

        @pl.when(index < hi)
        def _():
            pl.semaphore_signal(ready.at[hi], inc=1, device_id=at(index, lo, slab), device_id_type=MESH)

    edge_copy.start()
    for index in range(last):

        @pl.when(index < hi)
        def _():
            line_copy(index).start()

    @pl.when(lo == 0)
    def _():
        pl.semaphore_wait(pair_ready, 1)

    pair_copy(hi, act_hbm).start()

    @pl.when(hi < last)
    def _():
        pl.semaphore_wait(ready.at[hi + 1], 1)
        line_copy(hi + 1).start()

    for load in loads[1:]:
        load.wait()

    def build(which):
        view_index, tap = which // taps, which % taps
        start = starts_ref[tap, view_index : view_index + 1, :]
        turned = jnp.concatenate(
            [values_ref[which].astype(jnp.float32), jnp.zeros((8, width), jnp.float32)], axis=0
        )
        shift = 1
        while shift < 8:
            turned = jnp.where((start & shift) != 0, pltpu.roll(turned, shift, axis=0), turned)
            shift *= 2
        while shift < width:
            extra = min(shift, width - turned.shape[0])
            plain = jnp.concatenate([turned, jnp.zeros((extra, width), jnp.float32)], axis=0)
            moved = jnp.concatenate([jnp.zeros((shift, width), jnp.float32), turned], axis=0)[: plain.shape[0]]
            turned = jnp.where((start & shift) != 0, moved, plain)
            shift *= 2
        forward_w[tap * width : (tap + 1) * width, view_index * width : (view_index + 1) * width] = (
            turned.astype(jnp.bfloat16)
        )
        backward_w[view_index * width : (view_index + 1) * width, tap * width : (tap + 1) * width] = (
            turned.T.astype(jnp.bfloat16)
        )

    total = views * taps
    for which in range(total // 2):
        build(which)

    edge_copy.wait_recv()
    for index in range(last):

        @pl.when(index < hi)
        def _():
            line_edge_copy(index).start()

    pair_edge_copy(hi).start()

    @pl.when(hi < last)
    def _():
        line_edge_copy(hi + 1).start()

    for which in range(total // 2, total):
        build(which)

    for index in range(2, groups):

        @pl.when(index > hi + 1)
        def _():
            pl.semaphore_wait(ready.at[index], 1)
            line_copy(index).start()
            line_edge_copy(index).start()

    slice_at = lax.broadcasted_iota(jnp.int32, (group_rows, slices, width), 1)
    inner = jnp.where(slab == 0, slices - 1, 0)

    def halo_copy(step):
        return pltpu.make_async_remote_copy(
            src_ref=halo_out.at[step], dst_ref=halo_in.at[step],
            send_sem=halo_send.at[step], recv_sem=halo_recv.at[step],
            device_id=at(hi, lo, 1 - slab), device_id_type=MESH,
        )

    def part_copies(step):
        return [
            pltpu.make_async_remote_copy(
                src_ref=source.at[step], dst_ref=landing.at[step],
                send_sem=send.at[step], recv_sem=recv.at[step],
                device_id=at(hi, other, slab), device_id_type=MESH,
            )
            for source, landing, send, recv in (
                (part_unit, pair_unit, part_unit_send, part_unit_recv),
                (part_code, pair_code, part_send, part_recv),
            )
        ]

    def sum_copies(step, landing_at):
        return [
            pltpu.make_async_remote_copy(
                src_ref=source.at[step], dst_ref=landing.at[landing_at],
                send_sem=send.at[step], recv_sem=recv.at[landing_at],
                device_id=at(near(step), lo, slab), device_id_type=MESH,
            )
            for source, landing, send, recv in (
                (sum_unit, owner_unit, sum_unit_send, sum_unit_recv),
                (sum_code, owner_code, sum_send, sum_recv),
            )
        ]

    def relay(step):
        index = near(step)
        line_wait(index)
        pair_copy(index, block_of(index * PAIR + lo)).start()
        pair_edge_copy(index).start()

    def joined(step):
        for copy in part_copies(step):
            copy.wait_recv()
        return kept[step] + decode(pair_code[step], pair_unit[step])

    def pass_on(step):
        sum_code[step], sum_unit[step] = encode(joined(step))
        for copy in sum_copies(step, hi):
            copy.start()

    def one_group(step, carry):
        group = near(step)

        @pl.when(step < last)
        def _():
            relay(step + 1)

        pair_copy(group, block_of(group * PAIR + lo)).wait_recv()
        pair_edge_copy(group).wait_recv()
        blocks = acts[pl.ds(group * PAIR, PAIR)].astype(jnp.float32)
        image = blocks[:, :area].reshape(group_rows, slices, width)
        edge = blocks[:, area : area + rows].reshape(group_rows, 1, width)
        lower = jnp.where(slice_at == 0, jnp.where(slab == 0, 0.0, edge), pltpu.roll(image, 1, axis=1))
        upper = jnp.where(
            slice_at == slices - 1, jnp.where(slab == 0, edge, 0.0), pltpu.roll(image, slices - 1, axis=1)
        )
        stacked = jnp.concatenate(
            [x.reshape(-1, width).astype(jnp.bfloat16) for x in (lower, image, upper)], axis=1
        )
        summed = jnp.dot(stacked, forward_w[...], preferred_element_type=jnp.float32)
        counts_copy(step).wait()
        ratios = []
        ratio_edges = []
        for view_index in range(views):
            expected = (
                summed[:, view_index * width : (view_index + 1) * width].reshape(group_rows, slices, width)
                + back_ref[view_index].astype(jnp.float32)[None]
            )
            ratio = counts[step, view_index].astype(jnp.float32) / expected - 1.0
            ratio_edges.append(
                jnp.where(slab == 0, ratio[:, slices - 1, :], ratio[:, 0, :]).astype(jnp.bfloat16)
            )
            ratios.append(ratio.reshape(-1, width).astype(jnp.bfloat16))
        outer = pl.multiple_of((1 - slab) * ((taps - 1) * width), width)
        halo_out[step] = jnp.dot(
            jnp.concatenate(ratio_edges, axis=1), backward_w[:, pl.ds(outer, width)],
            preferred_element_type=jnp.float32,
        ).reshape(PAIR, rows, width)
        halo_copy(step).start()
        spread = jnp.dot(
            jnp.concatenate(ratios, axis=1), backward_w[...], preferred_element_type=jnp.float32
        ).reshape(group_rows, slices, taps * width)
        from_upper = pltpu.roll(spread[:, :, :width], slices - 1, axis=1)
        from_lower = pltpu.roll(spread[:, :, 2 * width :], 1, axis=1)
        from_upper = jnp.where(slice_at == slices - 1, 0.0, from_upper)
        from_lower = jnp.where(slice_at == 0, 0.0, from_lower)
        whole[...] = (spread[:, :, width : 2 * width] + from_upper + from_lower).reshape(
            PAIR, rows, slices, width
        )
        halo_copy(step).wait_recv()

        def with_halo(which):
            return whole[which] + jnp.where(
                slice_at[:rows] == inner, halo_in[step, which].reshape(rows, 1, width), 0.0
            )

        part_code[step], part_unit[step] = encode(with_halo(other))
        for copy in part_copies(step):
            copy.start()
        kept[step] = with_halo(lo)

        @pl.when(step > 1)
        def _():
            pass_on(step - 1)

        return carry

    lax.fori_loop(0, groups, one_group, 0)
    pass_on(last)
    out_ref[...] = joined(0)
    for step in range(1, groups):
        for copy in sum_copies(step, near(step)):
            copy.wait_recv()
        out_ref[...] += decode(owner_code[near(step)], owner_unit[near(step)])

    for index in range(groups):

        @pl.when(index != hi)
        def _():
            line_copy(index).wait_send()
            line_edge_copy(index).wait_send()

        pair_copy(index, act_hbm).wait_send()
        pair_edge_copy(index).wait_send()
    edge_copy.wait_send()
    for step in range(groups):
        halo_copy(step).wait_send()
        for copy in part_copies(step):
            copy.wait_send()
    for step in range(1, groups):
        for copy in sum_copies(step, hi):
            copy.wait_send()


def per_device(activity, histo_counts, background, blur_values, band_start):
    members = lax.axis_size("view")
    groups = members // PAIR
    rows, slices, width = activity.shape
    views, taps, _, band = blur_values.shape
    group_rows = PAIR * rows
    area = rows * slices
    dma = pltpu.SemaphoreType.DMA
    block = (rows, slices, width)
    vmem = pl.BlockSpec(memory_space=pltpu.VMEM)
    unit = (groups, 1, width)
    return pl.pallas_call(
        functools.partial(kernel, groups, rows),
        out_shape=jax.ShapeDtypeStruct(block, jnp.float32),
        in_specs=[pl.BlockSpec(memory_space=pl.ANY)] * 5,
        out_specs=vmem,
        scratch_shapes=[
            pltpu.VMEM(background.shape, jnp.bfloat16),
            pltpu.VMEM((views * taps, band, width), jnp.bfloat16),
            pltpu.VMEM((taps, views, width), jnp.int32),
            pltpu.VMEM((members, area + rows, width), jnp.bfloat16),
            pltpu.VMEM((rows, width), jnp.bfloat16),
            pltpu.VMEM((groups, views, group_rows, slices, width), jnp.int32),
            pltpu.VMEM((taps * width, views * width), jnp.bfloat16),
            pltpu.VMEM((views * width, taps * width), jnp.bfloat16),
            pltpu.VMEM((PAIR,) + block, jnp.float32),
            pltpu.VMEM((groups,) + block, jnp.float32),
            pltpu.VMEM((groups,) + block, jnp.int16),
            pltpu.VMEM(unit, jnp.float32),
            pltpu.VMEM((groups,) + block, jnp.int16),
            pltpu.VMEM(unit, jnp.float32),
            pltpu.VMEM((groups,) + block, jnp.int16),
            pltpu.VMEM(unit, jnp.float32),
            pltpu.VMEM((groups,) + block, jnp.int16),
            pltpu.VMEM(unit, jnp.float32),
            pltpu.VMEM((groups, PAIR, rows, width), jnp.float32),
            pltpu.VMEM((groups, PAIR, rows, width), jnp.float32),
            dma((4,)),
            dma((groups,)),
            pltpu.SemaphoreType.REGULAR((groups,)),
            pltpu.SemaphoreType.REGULAR,
            dma((groups,)), dma((groups,)), dma((groups,)), dma((groups,)),
            dma((groups,)), dma((groups,)), dma((groups,)), dma((groups,)),
            dma, dma,
            dma((groups,)), dma((groups,)),
            dma((groups,)), dma((groups,)), dma((groups,)), dma((groups,)),
            dma((groups,)), dma((groups,)), dma((groups,)), dma((groups,)),
        ],
        compiler_params=pltpu.CompilerParams(collective_id=0, has_side_effects=True, vmem_limit_bytes=VMEM_LIMIT),
        name="poisson_gradient",
    )(
        activity.reshape(area, width), histo_counts, background,
        jnp.swapaxes(blur_values, 2, 3).reshape(views * taps, band, width), jnp.swapaxes(band_start, 0, 1),
    )


def solution(mesh):
    placed = (
        P(("parts", "view"), "slab", None),
        P(("parts", "view"), None, "slab", None),
        P(("parts", "view"), "slab", None),
        P("view", None, None, None),
        P("view", None, None),
    )
    return jax.shard_map(
        per_device,
        mesh=mesh,
        in_specs=placed,
        out_specs=P(("parts", "view"), "slab", None),
        check_vma=False,
    )
```

time: 31.3 us -> 34.1 us (1.089)
  Pallas kernels: 29.6 us -> 32.4 us
    pallas_call x1, Pallas kernels: 29.6 us -> 32.4 us  [per_device(): pl.pallas_call(functools.partial(kernel, groups, rows), out_shape=jax.Sha...]
where the time goes in v1:
time: 34.1 us; the launch traced here: 34 us
  Pallas kernels  32.4 us (95%)
  local copies, waits for them, and re-layouts  1.57 us (5%)
    pallas_call x1, Pallas kernels, per_device(): pl.pallas_call(functools.partial(kernel, groups, rows), out_shape=jax.Sha...  32.4 us
    unnamed x1, local copies, waits for them, and re-layouts  1.57 us

profile of v1, /device:TPU:0, one launch (start us, length us, event | category | flops | bytes accessed | tf_op | source)
XLA Modules:
  0.0 34.0 jit_solution(16893903829530837458)
XLA Ops:
  0.0 32.4 %poisson_gradient.1 = f32[8,16,256]{2,1,0:T(8,128)} custom-call(bf16[128,256]{1,0:T(8,128)(2,1)} %bitcast.6, s32[2,64,16,256]{3,2,1,0:T(8,128)} %counts_hbm.1, bf16[2,16,256]{2,1,0:T(8,128)(2,1)} %back_hbm.1, bf16[6,32,256]{2,1,0:T(8,128)(2,1)} %bitcast.5, s32[3,2,256]{2,1,0:T(2,128)} %bitcast.7), custom_call_target="tpu_custom_call" | custom-call | tf_op jit(solution)/shard_map/poisson_gradient/pallas_call | solution.py:387
  32.4 1.6 %copy.7 = f32[8,16,256]{2,1,0:T(8,128)} copy(f32[8,16,256]{2,1,0:T(8,128)} %poisson_gradient.1) | data formatting | bytes 262144

commit v2 on v1

v2 whole, which is shorter than its diff:
```python
import functools

import jax
import jax.numpy as jnp
from jax import lax
from jax.experimental import pallas as pl
from jax.experimental.pallas import tpu as pltpu
from jax.sharding import PartitionSpec as P

MESH = pl.DeviceIdType.MESH
PAIR = 2


CODE_MAX = 32767.0
TINY = 1e-30
VMEM_LIMIT = 63 << 20


def encode(block):
    top = jnp.max(jnp.abs(block), axis=(0, 1), keepdims=False)[None, :]
    scale = jnp.where(top > TINY, CODE_MAX / jnp.maximum(top, TINY), 0.0)
    code = jnp.round(block * scale[None]).astype(jnp.int32).astype(jnp.int16)
    return code, top * (1.0 / CODE_MAX)


def decode(code, unit):
    return code.astype(jnp.int32).astype(jnp.float32) * unit[None]


def kernel(
    groups, act_hbm, counts_hbm, back_hbm, values_hbm, starts_hbm, out_ref,
    back_ref, values_ref, starts_ref,
    acts, edge_own, counts, counts_raw, counts_out, counts_in, forward_w, backward_w, whole,
    sum_code, sum_unit, owner_code, owner_unit, halo_out, halo_in,
    load_sem, counts_sem, raw_sem, ready, pair_ready, line_send, line_recv, line_edge_send, line_edge_recv,
    swap_send, swap_recv, share_send, share_recv, trade_send, trade_recv,
    edge_send, edge_recv, halo_send, halo_recv, sum_send, sum_recv, sum_unit_send, sum_unit_recv,
):
    part = lax.axis_index("parts")
    view = lax.axis_index("view")
    slab = lax.axis_index("slab")
    last = groups - 1
    hi = view // PAIR
    lo = view % PAIR
    other = 1 - lo
    rows, slices, width = out_ref.shape
    area = rows * slices
    views = back_hbm.shape[0]
    total = values_hbm.shape[0]
    taps = total // views
    half = total // 2

    def at(hi_index, lo_index, slab_index):
        return (part, hi_index * PAIR + lo_index, slab_index)

    def cross(first, second):
        index, unit = 0, 1
        while unit < groups:
            index += ((first // unit + second // unit) % 2) * unit
            unit *= 2
        return index

    def met(step):
        return cross(hi, (groups - step) % groups)

    def step_of(index):
        return (groups - cross(hi, index)) % groups

    barrier = pltpu.get_barrier_semaphore()
    pl.semaphore_signal(barrier, inc=1, device_id=at(hi, lo, 1 - slab), device_id_type=MESH)

    @pl.when(lo == 0)
    def _():
        pl.semaphore_signal(barrier, inc=1, device_id=at(hi, 1, slab), device_id_type=MESH)

    for index in range(1, groups):

        @pl.when(index > hi)
        def _():
            pl.semaphore_signal(barrier, inc=1, device_id=at(index, lo, slab), device_id_type=MESH)

    def counts_copy(step, column, target, sems):
        first = pl.multiple_of((met(step) * PAIR + column) * rows, rows)
        return pltpu.make_async_copy(counts_hbm.at[:, pl.ds(first, rows)], target.at[step], sems.at[step])

    def block_of(index):
        return acts.at[index, pl.ds(0, area)]

    def edge_of(index):
        return acts.at[index, pl.ds(area, rows)]

    loads = [
        pltpu.make_async_copy(source, target, load_sem.at[index])
        for index, (source, target) in enumerate(
            (
                (act_hbm, block_of(hi)), (values_hbm, values_ref.at[pl.ds(0, total)]),
                (starts_hbm, starts_ref.at[0]), (back_hbm, back_ref.at[0]),
            )
        )
    ]
    order = list(range(1, groups)) + [0]
    loads[0].start()
    for step in order:
        counts_copy(step, other, counts_raw, raw_sem).start()
    for load in loads[1:]:
        load.start()
    for step in order:
        counts_copy(step, lo, counts, counts_sem).start()

    pl.semaphore_wait(barrier, 1 + hi + lo)

    @pl.when(lo == 1)
    def _():
        pl.semaphore_signal(pair_ready, inc=1, device_id=at(hi, 0, slab), device_id_type=MESH)

    for reach in range(1, groups):

        @pl.when(hi >= reach)
        def _():
            target = jnp.maximum(hi - reach, 0)
            pl.semaphore_signal(
                ready.at[step_of(target)], inc=1, device_id=at(target, lo, slab), device_id_type=MESH
            )

    def line_copies(step):
        return [
            pltpu.make_async_remote_copy(
                src_ref=piece, dst_ref=piece, send_sem=send.at[step], recv_sem=recv.at[step],
                device_id=at(met(step), lo, slab), device_id_type=MESH,
            )
            for piece, send, recv in (
                (block_of(hi), line_send, line_recv), (edge_of(hi), line_edge_send, line_edge_recv)
            )
        ]

    def to_pair(source, target, send, recv):
        return pltpu.make_async_remote_copy(
            src_ref=source, dst_ref=target, send_sem=send, recv_sem=recv,
            device_id=at(hi, other, slab), device_id_type=MESH,
        )

    def to_core(source, target, send, recv):
        return pltpu.make_async_remote_copy(
            src_ref=source, dst_ref=target, send_sem=send, recv_sem=recv,
            device_id=at(hi, lo, 1 - slab), device_id_type=MESH,
        )

    landed = values_ref.at[pl.ds(total + slab * half, half)]
    swaps = [
        to_pair(source, target, swap_send.at[index], swap_recv.at[index])
        for index, (source, target) in enumerate(
            (
                (values_hbm.at[pl.ds(slab * half, half)], landed),
                (starts_hbm, starts_ref.at[1]), (back_hbm, back_ref.at[1]),
            )
        )
    ]
    share = to_core(landed, landed, share_send, share_recv)
    edge_copy = to_core(edge_own, edge_of(hi), edge_send, edge_recv)

    def trade(step):
        return to_pair(counts_out.at[step], counts_in.at[step], trade_send.at[step], trade_recv.at[step])

    def halo_copy(step):
        return to_core(halo_out.at[step], halo_in.at[step], halo_send.at[step], halo_recv.at[step])

    def sum_copies(step):
        return [
            pltpu.make_async_remote_copy(
                src_ref=source.at[step], dst_ref=landing.at[step],
                send_sem=send.at[step], recv_sem=recv.at[step],
                device_id=at(met(step), lo, slab), device_id_type=MESH,
            )
            for source, landing, send, recv in (
                (sum_unit, owner_unit, sum_unit_send, sum_unit_recv),
                (sum_code, owner_code, sum_send, sum_recv),
            )
        ]

    loads[0].wait()
    for reach in range(groups - 1, 0, -1):

        @pl.when(hi >= reach)
        def _():
            line_copies(step_of(jnp.maximum(hi - reach, 0)))[0].start()

    own = acts[hi, :area].astype(jnp.float32).reshape(rows, slices, width)
    edge_own[...] = jnp.where(slab == 0, own[:, slices - 1, :], own[:, 0, :]).astype(jnp.bfloat16)
    edge_copy.start()

    @pl.when(lo == 0)
    def _():
        pl.semaphore_wait(pair_ready, 1)

    for copy in swaps:
        copy.start()

    def send_counts(step):
        counts_copy(step, other, counts_raw, raw_sem).wait()
        counts_out[step] = counts_raw[step].astype(jnp.float32).astype(jnp.bfloat16)
        trade(step).start()

    send_counts(order[0])

    @pl.when(hi < last)
    def _():
        nearest = step_of(jnp.minimum(hi + 1, last))
        pl.semaphore_wait(ready.at[nearest], 1)
        line_copies(nearest)[0].start()

    edge_copy.wait_recv()
    for reach in range(groups - 1, 0, -1):

        @pl.when(hi >= reach)
        def _():
            line_copies(step_of(jnp.maximum(hi - reach, 0)))[1].start()

    @pl.when(hi < last)
    def _():
        line_copies(step_of(jnp.minimum(hi + 1, last)))[1].start()

    def send_rest(place, carry):
        send_counts(lax.rem(place + 1, groups))
        return carry

    lax.fori_loop(1, groups, send_rest, 0)

    def build(which, slot):
        view_index, tap = which // taps, which % taps
        start = starts_ref[slot, tap, view_index : view_index + 1, :]
        turned = jnp.concatenate(
            [values_ref[slot * total + which].astype(jnp.float32), jnp.zeros((8, width), jnp.float32)], axis=0
        )
        shift = 1
        while shift < 8:
            turned = jnp.where((start & shift) != 0, pltpu.roll(turned, shift, axis=0), turned)
            shift *= 2
        while shift < width:
            extra = min(shift, width - turned.shape[0])
            plain = jnp.concatenate([turned, jnp.zeros((extra, width), jnp.float32)], axis=0)
            moved = jnp.concatenate([jnp.zeros((shift, width), jnp.float32), turned], axis=0)[: plain.shape[0]]
            turned = jnp.where((start & shift) != 0, moved, plain)
            shift *= 2
        across = slot * views + view_index
        forward_w[tap * width : (tap + 1) * width, across * width : (across + 1) * width] = (
            turned.astype(jnp.bfloat16)
        )
        backward_w[across * width : (across + 1) * width, tap * width : (tap + 1) * width] = (
            turned.T.astype(jnp.bfloat16)
        )

    for load in loads[1:]:
        load.wait()
    for which in range(total):
        build(which, 0)
    for reach in range(2, groups):

        @pl.when(hi + reach <= last)
        def _():
            later = step_of(jnp.minimum(hi + reach, last))
            pl.semaphore_wait(ready.at[later], 1)
            for copy in line_copies(later):
                copy.start()

    for copy in swaps:
        copy.wait_recv()
    share.start()
    share.wait_recv()
    for which in range(total):
        build(which, 1)

    slice_at = lax.broadcasted_iota(jnp.int32, (rows, slices, width), 1)
    inner = jnp.where(slab == 0, slices - 1, 0)

    def one_group(place, carry):
        step = lax.rem(place + 1, groups)
        group = met(step)

        @pl.when(step > 0)
        def _():
            for copy in line_copies(step):
                copy.wait_recv()

        block = acts[group].astype(jnp.float32)
        image = block[:area].reshape(rows, slices, width)
        edge = block[area:].reshape(rows, 1, width)
        lower = jnp.where(slice_at == 0, jnp.where(slab == 0, 0.0, edge), pltpu.roll(image, 1, axis=1))
        upper = jnp.where(
            slice_at == slices - 1, jnp.where(slab == 0, edge, 0.0), pltpu.roll(image, slices - 1, axis=1)
        )
        stacked = jnp.concatenate(
            [x.reshape(-1, width).astype(jnp.bfloat16) for x in (lower, image, upper)], axis=1
        )
        summed = jnp.dot(stacked, forward_w[...], preferred_element_type=jnp.float32)
        counts_copy(step, lo, counts, counts_sem).wait()
        trade(step).wait_recv()
        ratios = []
        ratio_edges = []
        for across in range(PAIR * views):
            slot, view_index = across // views, across % views
            expected = (
                summed[:, across * width : (across + 1) * width].reshape(rows, slices, width)
                + back_ref[slot, view_index].astype(jnp.float32)[None]
            )
            events = (counts_in if slot else counts)[step, view_index].astype(jnp.float32)
            ratio = events / expected - 1.0
            ratio_edges.append(
                jnp.where(slab == 0, ratio[:, slices - 1, :], ratio[:, 0, :]).astype(jnp.bfloat16)
            )
            ratios.append(ratio.reshape(-1, width).astype(jnp.bfloat16))
        outer = pl.multiple_of((1 - slab) * ((taps - 1) * width), width)
        halo_out[step] = jnp.dot(
            jnp.concatenate(ratio_edges, axis=1), backward_w[:, pl.ds(outer, width)],
            preferred_element_type=jnp.float32,
        )
        halo_copy(step).start()
        spread = jnp.dot(
            jnp.concatenate(ratios, axis=1), backward_w[...], preferred_element_type=jnp.float32
        ).reshape(rows, slices, taps * width)
        from_upper = pltpu.roll(spread[:, :, :width], slices - 1, axis=1)
        from_lower = pltpu.roll(spread[:, :, 2 * width :], 1, axis=1)
        from_upper = jnp.where(slice_at == slices - 1, 0.0, from_upper)
        from_lower = jnp.where(slice_at == 0, 0.0, from_lower)
        whole[...] = spread[:, :, width : 2 * width] + from_upper + from_lower
        halo_copy(step).wait_recv()
        whole[...] += jnp.where(slice_at == inner, halo_in[step].reshape(rows, 1, width), 0.0)

        @pl.when(step > 0)
        def _():
            sum_code[step], sum_unit[step] = encode(whole[...])
            for copy in sum_copies(step):
                copy.start()

        return carry

    lax.fori_loop(0, groups, one_group, 0)
    for step in range(1, groups):
        for copy in sum_copies(step):
            copy.wait_recv()
        whole[...] += decode(owner_code[step], owner_unit[step])
    out_ref[...] = whole[...]

    for copy in swaps:
        copy.wait_send()
    share.wait_send()
    edge_copy.wait_send()
    for step in range(groups):
        halo_copy(step).wait_send()
        trade(step).wait_send()
    for step in range(1, groups):
        for copy in line_copies(step) + sum_copies(step):
            copy.wait_send()


def per_device(activity, histo_counts, background, blur_values, band_start):
    members = lax.axis_size("view")
    groups = members // PAIR
    rows, slices, width = activity.shape
    views, taps, _, band = blur_values.shape
    area = rows * slices
    total = views * taps
    dma = pltpu.SemaphoreType.DMA
    block = (rows, slices, width)
    shared = (groups, views) + block
    unit = (groups, 1, width)
    return pl.pallas_call(
        functools.partial(kernel, groups),
        out_shape=jax.ShapeDtypeStruct(block, jnp.float32),
        in_specs=[pl.BlockSpec(memory_space=pl.ANY)] * 5,
        out_specs=pl.BlockSpec(memory_space=pltpu.VMEM),
        scratch_shapes=[
            pltpu.VMEM((PAIR,) + background.shape, jnp.bfloat16),
            pltpu.VMEM((PAIR * total, band, width), jnp.bfloat16),
            pltpu.VMEM((PAIR, taps, views, width), jnp.int32),
            pltpu.VMEM((groups, area + rows, width), jnp.bfloat16),
            pltpu.VMEM((rows, width), jnp.bfloat16),
            pltpu.VMEM(shared, jnp.int32),
            pltpu.VMEM(shared, jnp.int32),
            pltpu.VMEM(shared, jnp.bfloat16),
            pltpu.VMEM(shared, jnp.bfloat16),
            pltpu.VMEM((taps * width, PAIR * views * width), jnp.bfloat16),
            pltpu.VMEM((PAIR * views * width, taps * width), jnp.bfloat16),
            pltpu.VMEM(block, jnp.float32),
            pltpu.VMEM((groups,) + block, jnp.int16),
            pltpu.VMEM(unit, jnp.float32),
            pltpu.VMEM((groups,) + block, jnp.int16),
            pltpu.VMEM(unit, jnp.float32),
            pltpu.VMEM((groups, rows, width), jnp.float32),
            pltpu.VMEM((groups, rows, width), jnp.float32),
            dma((4,)),
            dma((groups,)), dma((groups,)),
            pltpu.SemaphoreType.REGULAR((groups,)),
            pltpu.SemaphoreType.REGULAR,
            dma((groups,)), dma((groups,)), dma((groups,)), dma((groups,)),
            dma((3,)), dma((3,)), dma, dma, dma((groups,)), dma((groups,)),
            dma, dma, dma((groups,)), dma((groups,)),
            dma((groups,)), dma((groups,)), dma((groups,)), dma((groups,)),
        ],
        compiler_params=pltpu.CompilerParams(collective_id=0, has_side_effects=True, vmem_limit_bytes=VMEM_LIMIT),
        name="poisson_gradient",
    )(
        activity.reshape(area, width), histo_counts, background,
        jnp.swapaxes(blur_values, 2, 3).reshape(total, band, width), jnp.swapaxes(band_start, 0, 1),
    )


def solution(mesh):
    placed = (
        P(("parts", "view"), "slab", None),
        P(("parts", "view"), None, "slab", None),
        P(("parts", "view"), "slab", None),
        P("view", None, None, None),
        P("view", None, None),
    )
    return jax.shard_map(
        per_device,
        mesh=mesh,
        in_specs=placed,
        out_specs=P(("parts", "view"), "slab", None),
        check_vma=False,
    )
```

time: 34.1 us -> 24.7 us (0.72)
  Pallas kernels: 32.4 us -> 23 us
    pallas_call x1, Pallas kernels: 32.4 us -> 23 us  [per_device(): pl.pallas_call(functools.partial(kernel, groups), out_shape=jax.ShapeDtyp...]
where the time goes in v2:
time: 24.7 us; the launch traced here: 24.6 us
  Pallas kernels  23 us (93%)
  local copies, waits for them, and re-layouts  1.57 us (6%)
    pallas_call x1, Pallas kernels, per_device(): pl.pallas_call(functools.partial(kernel, groups), out_shape=jax.ShapeDtyp...  23 us
    unnamed x1, local copies, waits for them, and re-layouts  1.57 us

profile of v2, /device:TPU:0, one launch (start us, length us, event | category | flops | bytes accessed | tf_op | source)
XLA Modules:
  0.0 24.6 jit_solution(4487367913666514963)
XLA Ops:
  0.0 23.0 %poisson_gradient.1 = f32[8,16,256]{2,1,0:T(8,128)} custom-call(bf16[128,256]{1,0:T(8,128)(2,1)} %bitcast.6, s32[2,64,16,256]{3,2,1,0:T(8,128)} %counts_hbm.1, bf16[2,16,256]{2,1,0:T(8,128)(2,1)} %back_hbm.1, bf16[6,32,256]{2,1,0:T(8,128)(2,1)} %bitcast.5, s32[3,2,256]{2,1,0:T(2,128)} %bitcast.7), custom_call_target="tpu_custom_call" | custom-call | tf_op jit(solution)/shard_map/poisson_gradient/pallas_call | solution.py:366
  23.0 1.6 %copy.7 = f32[8,16,256]{2,1,0:T(8,128)} copy(f32[8,16,256]{2,1,0:T(8,128)} %poisson_gradient.1) | data formatting | bytes 262144

commit v3 on v2

v3 whole, which is shorter than its diff:
```python
import functools

import jax
import jax.numpy as jnp
from jax import lax
from jax.experimental import pallas as pl
from jax.experimental.pallas import tpu as pltpu
from jax.sharding import PartitionSpec as P

MESH = pl.DeviceIdType.MESH
PAIR = 2


CODE_MAX = 32767.0
TINY = 1e-30
VMEM_LIMIT = 63 << 20


def encode(block):
    top = jnp.max(jnp.abs(block), axis=(0, 1), keepdims=False)[None, :]
    scale = jnp.where(top > TINY, CODE_MAX / jnp.maximum(top, TINY), 0.0)
    code = jnp.round(block * scale[None]).astype(jnp.int32).astype(jnp.int16)
    return code, top * (1.0 / CODE_MAX)


def decode(code, unit):
    return code.astype(jnp.int32).astype(jnp.float32) * unit[None]


def kernel(
    groups, act_hbm, counts_hbm, back_hbm, values_hbm, starts_hbm, out_ref,
    back_ref, values_ref, starts_ref,
    acts, edge_own, counts, counts_raw, counts_out, counts_in, forward_w, backward_w, summed, spread_own, whole,
    sum_code, sum_unit, owner_code, owner_unit, halo_out, halo_in,
    load_sem, counts_sem, raw_sem, ready, pair_ready, line_send, line_recv, line_edge_send, line_edge_recv,
    swap_send, swap_recv, share_send, share_recv, trade_send, trade_recv,
    edge_send, edge_recv, halo_send, halo_recv, sum_send, sum_recv, sum_unit_send, sum_unit_recv,
):
    part = lax.axis_index("parts")
    view = lax.axis_index("view")
    slab = lax.axis_index("slab")
    last = groups - 1
    hi = view // PAIR
    lo = view % PAIR
    other = 1 - lo
    rows, slices, width = out_ref.shape
    area = rows * slices
    views = back_hbm.shape[0]
    total = values_hbm.shape[0]
    taps = total // views
    half = total // 2

    def at(hi_index, lo_index, slab_index):
        return (part, hi_index * PAIR + lo_index, slab_index)

    def group_at(place):
        return jnp.where(place == last, hi, jnp.where(place < hi, place, place + 1))

    barrier = pltpu.get_barrier_semaphore()
    pl.semaphore_signal(barrier, inc=1, device_id=at(hi, lo, 1 - slab), device_id_type=MESH)

    @pl.when(lo == 0)
    def _():
        pl.semaphore_signal(barrier, inc=1, device_id=at(hi, 1, slab), device_id_type=MESH)

    for index in range(1, groups):

        @pl.when(index > hi)
        def _():
            pl.semaphore_signal(barrier, inc=1, device_id=at(index, lo, slab), device_id_type=MESH)

    def counts_copy(place, column, target, sems):
        first = pl.multiple_of((group_at(place) * PAIR + column) * rows, rows)
        return pltpu.make_async_copy(counts_hbm.at[:, pl.ds(first, rows)], target.at[place], sems.at[place])

    def block_of(index):
        return acts.at[index, pl.ds(0, area)]

    def edge_of(index):
        return acts.at[index, pl.ds(area, rows)]

    loads = [
        pltpu.make_async_copy(source, target, load_sem.at[index])
        for index, (source, target) in enumerate(
            (
                (act_hbm, block_of(hi)), (values_hbm, values_ref.at[pl.ds(0, total)]),
                (starts_hbm, starts_ref.at[0]), (back_hbm, back_ref.at[0]),
            )
        )
    ]
    loads[0].start()
    for place in range(groups):
        counts_copy(place, other, counts_raw, raw_sem).start()
    for load in loads[1:]:
        load.start()
    for place in range(groups):
        counts_copy(place, lo, counts, counts_sem).start()

    pl.semaphore_wait(barrier, 1 + hi + lo)

    @pl.when(lo == 1)
    def _():
        pl.semaphore_signal(pair_ready, inc=1, device_id=at(hi, 0, slab), device_id_type=MESH)

    for target in range(last):

        @pl.when(target < hi)
        def _():
            pl.semaphore_signal(ready.at[hi], inc=1, device_id=at(target, lo, slab), device_id_type=MESH)

    def line_copy(target, piece, send, recv, source):
        return pltpu.make_async_remote_copy(
            src_ref=piece(hi), dst_ref=piece(hi), send_sem=send.at[target], recv_sem=recv.at[source],
            device_id=at(target, lo, slab), device_id_type=MESH,
        )

    def block_copy(target, source=hi):
        return line_copy(target, block_of, line_send, line_recv, source)

    def rim_copy(target, source=hi):
        return line_copy(target, edge_of, line_edge_send, line_edge_recv, source)

    def to_pair(source, target, send, recv):
        return pltpu.make_async_remote_copy(
            src_ref=source, dst_ref=target, send_sem=send, recv_sem=recv,
            device_id=at(hi, other, slab), device_id_type=MESH,
        )

    def to_core(source, target, send, recv):
        return pltpu.make_async_remote_copy(
            src_ref=source, dst_ref=target, send_sem=send, recv_sem=recv,
            device_id=at(hi, lo, 1 - slab), device_id_type=MESH,
        )

    landed = values_ref.at[pl.ds(total + slab * half, half)]
    swaps = [
        to_pair(source, target, swap_send.at[index], swap_recv.at[index])
        for index, (source, target) in enumerate(
            (
                (values_hbm.at[pl.ds(slab * half, half)], landed),
                (starts_hbm, starts_ref.at[1]), (back_hbm, back_ref.at[1]),
            )
        )
    ]
    share = to_core(landed, landed, share_send, share_recv)
    edge_copy = to_core(edge_own, edge_of(hi), edge_send, edge_recv)

    def trade(place):
        return to_pair(counts_out.at[place], counts_in.at[place], trade_send.at[place], trade_recv.at[place])

    def halo_copy(place):
        return to_core(halo_out.at[place], halo_in.at[place], halo_send.at[place], halo_recv.at[place])

    def sum_copies(target, source=hi):
        return [
            pltpu.make_async_remote_copy(
                src_ref=out.at[target], dst_ref=landing.at[hi], send_sem=send.at[target], recv_sem=recv.at[source],
                device_id=at(target, lo, slab), device_id_type=MESH,
            )
            for out, landing, send, recv in (
                (sum_unit, owner_unit, sum_unit_send, sum_unit_recv),
                (sum_code, owner_code, sum_send, sum_recv),
            )
        ]

    @pl.when(lo == 1)
    def _():
        for copy in swaps:
            copy.start()

    loads[0].wait()
    for target in range(last):

        @pl.when(target < hi)
        def _():
            block_copy(target).start()

    own = acts[hi, :area].astype(jnp.float32).reshape(rows, slices, width)
    edge_own[...] = jnp.where(slab == 0, own[:, slices - 1, :], own[:, 0, :]).astype(jnp.bfloat16)
    edge_copy.start()

    def send_counts(place):
        counts_copy(place, other, counts_raw, raw_sem).wait()
        counts_out[place] = counts_raw[place].astype(jnp.float32).astype(jnp.bfloat16)
        trade(place).start()

    @pl.when(lo == 0)
    def _():
        pl.semaphore_wait(pair_ready, 1)
        for copy in swaps:
            copy.start()

    send_counts(0)

    @pl.when(hi < last)
    def _():
        pl.semaphore_wait(ready.at[hi + 1], 1)
        block_copy(hi + 1).start()

    edge_copy.wait_recv()
    for target in range(last):

        @pl.when(target < hi)
        def _():
            rim_copy(target).start()

    @pl.when(hi < last)
    def _():
        rim_copy(hi + 1).start()

    def send_rest(place, carry):
        send_counts(place)
        return carry

    lax.fori_loop(1, groups, send_rest, 0)

    def build(which, slot):
        view_index, tap = which // taps, which % taps
        start = starts_ref[slot, tap, view_index : view_index + 1, :]
        turned = jnp.concatenate(
            [values_ref[slot * total + which].astype(jnp.float32), jnp.zeros((8, width), jnp.float32)], axis=0
        )
        shift = 1
        while shift < 8:
            turned = jnp.where((start & shift) != 0, pltpu.roll(turned, shift, axis=0), turned)
            shift *= 2
        while shift < width:
            extra = min(shift, width - turned.shape[0])
            plain = jnp.concatenate([turned, jnp.zeros((extra, width), jnp.float32)], axis=0)
            moved = jnp.concatenate([jnp.zeros((shift, width), jnp.float32), turned], axis=0)[: plain.shape[0]]
            turned = jnp.where((start & shift) != 0, moved, plain)
            shift *= 2
        place = slot * views + view_index
        forward_w[tap * width : (tap + 1) * width, place * width : (place + 1) * width] = (
            turned.astype(jnp.bfloat16)
        )
        backward_w[place * width : (place + 1) * width, tap * width : (tap + 1) * width] = (
            turned.T.astype(jnp.bfloat16)
        )

    for load in loads[1:]:
        load.wait()
    for which in range(total):
        build(which, 0)
    for target in range(2, groups):

        @pl.when(target > hi + 1)
        def _():
            pl.semaphore_wait(ready.at[target], 1)
            block_copy(target).start()
            rim_copy(target).start()

    for copy in swaps:
        copy.wait_recv()
    share.start()
    share.wait_recv()
    for which in range(total):
        build(which, 1)

    slice_at = lax.broadcasted_iota(jnp.int32, (rows, slices, width), 1)
    inner = jnp.where(slab == 0, slices - 1, 0)

    across = views * width
    outer = pl.multiple_of((1 - slab) * ((taps - 1) * width), width)

    def one_group(place, carry):
        group = group_at(place)

        @pl.when(place < last)
        def _():
            block_copy(group, group).wait_recv()
            rim_copy(group, group).wait_recv()

        block = acts[group].astype(jnp.float32)
        image = block[:area].reshape(rows, slices, width)
        edge = block[area:].reshape(rows, 1, width)
        lower = jnp.where(slice_at == 0, jnp.where(slab == 0, 0.0, edge), pltpu.roll(image, 1, axis=1))
        upper = jnp.where(
            slice_at == slices - 1, jnp.where(slab == 0, edge, 0.0), pltpu.roll(image, slices - 1, axis=1)
        )
        stacked = jnp.concatenate(
            [x.reshape(-1, width).astype(jnp.bfloat16) for x in (lower, image, upper)], axis=1
        )
        summed[...] = jnp.dot(stacked, forward_w[...], preferred_element_type=jnp.float32)

        def ratios_of(slot, events):
            ratios = []
            ratio_edges = []
            for view_index in range(views):
                first = slot * across + view_index * width
                expected = (
                    summed[:, first : first + width].reshape(rows, slices, width)
                    + back_ref[slot, view_index].astype(jnp.float32)[None]
                )
                ratio = events[place, view_index].astype(jnp.float32) / expected - 1.0
                ratio_edges.append(
                    jnp.where(slab == 0, ratio[:, slices - 1, :], ratio[:, 0, :]).astype(jnp.bfloat16)
                )
                ratios.append(ratio.reshape(-1, width).astype(jnp.bfloat16))
            return jnp.concatenate(ratios, axis=1), jnp.concatenate(ratio_edges, axis=1)

        counts_copy(place, lo, counts, counts_sem).wait()
        ratios, ratio_edges = ratios_of(0, counts)
        halo_out[place] = jnp.dot(
            ratio_edges, backward_w[:across, pl.ds(outer, width)], preferred_element_type=jnp.float32
        )
        spread_own[...] = jnp.dot(ratios, backward_w[:across], preferred_element_type=jnp.float32)
        trade(place).wait_recv()
        ratios, ratio_edges = ratios_of(1, counts_in)
        halo_out[place] += jnp.dot(
            ratio_edges, backward_w[across:, pl.ds(outer, width)], preferred_element_type=jnp.float32
        )
        halo_copy(place).start()
        spread = (
            spread_own[...] + jnp.dot(ratios, backward_w[across:], preferred_element_type=jnp.float32)
        ).reshape(rows, slices, taps * width)
        from_upper = pltpu.roll(spread[:, :, :width], slices - 1, axis=1)
        from_lower = pltpu.roll(spread[:, :, 2 * width :], 1, axis=1)
        from_upper = jnp.where(slice_at == slices - 1, 0.0, from_upper)
        from_lower = jnp.where(slice_at == 0, 0.0, from_lower)
        whole[...] = spread[:, :, width : 2 * width] + from_upper + from_lower
        halo_copy(place).wait_recv()
        whole[...] += jnp.where(slice_at == inner, halo_in[place].reshape(rows, 1, width), 0.0)

        @pl.when(place < last)
        def _():
            sum_code[group], sum_unit[group] = encode(whole[...])
            for copy in sum_copies(group):
                copy.start()

        return carry

    lax.fori_loop(0, groups, one_group, 0)
    for place in range(last):
        source = group_at(place)
        for copy in sum_copies(source, source):
            copy.wait_recv()
        whole[...] += decode(owner_code[source], owner_unit[source])
    out_ref[...] = whole[...]

    for copy in swaps:
        copy.wait_send()
    share.wait_send()
    edge_copy.wait_send()
    for place in range(groups):
        halo_copy(place).wait_send()
        trade(place).wait_send()
    for place in range(last):
        target = group_at(place)
        block_copy(target).wait_send()
        rim_copy(target).wait_send()
        for copy in sum_copies(target):
            copy.wait_send()


def per_device(activity, histo_counts, background, blur_values, band_start):
    members = lax.axis_size("view")
    groups = members // PAIR
    rows, slices, width = activity.shape
    views, taps, _, band = blur_values.shape
    area = rows * slices
    total = views * taps
    dma = pltpu.SemaphoreType.DMA
    block = (rows, slices, width)
    shared = (groups, views) + block
    unit = (groups, 1, width)
    return pl.pallas_call(
        functools.partial(kernel, groups),
        out_shape=pltpu.VMEM(block, jnp.float32),
        in_specs=[pl.BlockSpec(memory_space=pl.ANY)] * 5,
        out_specs=pl.BlockSpec(memory_space=pltpu.VMEM),
        scratch_shapes=[
            pltpu.VMEM((PAIR,) + background.shape, jnp.bfloat16),
            pltpu.VMEM((PAIR * total, band, width), jnp.bfloat16),
            pltpu.VMEM((PAIR, taps, views, width), jnp.int32),
            pltpu.VMEM((groups, area + rows, width), jnp.bfloat16),
            pltpu.VMEM((rows, width), jnp.bfloat16),
            pltpu.VMEM(shared, jnp.int32),
            pltpu.VMEM(shared, jnp.int32),
            pltpu.VMEM(shared, jnp.bfloat16),
            pltpu.VMEM(shared, jnp.bfloat16),
            pltpu.VMEM((taps * width, PAIR * views * width), jnp.bfloat16),
            pltpu.VMEM((PAIR * views * width, taps * width), jnp.bfloat16),
            pltpu.VMEM((area, PAIR * views * width), jnp.float32),
            pltpu.VMEM((area, taps * width), jnp.float32),
            pltpu.VMEM(block, jnp.float32),
            pltpu.VMEM((groups,) + block, jnp.int16),
            pltpu.VMEM(unit, jnp.float32),
            pltpu.VMEM((groups,) + block, jnp.int16),
            pltpu.VMEM(unit, jnp.float32),
            pltpu.VMEM((groups, rows, width), jnp.float32),
            pltpu.VMEM((groups, rows, width), jnp.float32),
            dma((4,)),
            dma((groups,)), dma((groups,)),
            pltpu.SemaphoreType.REGULAR((groups,)),
            pltpu.SemaphoreType.REGULAR,
            dma((groups,)), dma((groups,)), dma((groups,)), dma((groups,)),
            dma((3,)), dma((3,)), dma, dma, dma((groups,)), dma((groups,)),
            dma, dma, dma((groups,)), dma((groups,)),
            dma((groups,)), dma((groups,)), dma((groups,)), dma((groups,)),
        ],
        compiler_params=pltpu.CompilerParams(collective_id=0, has_side_effects=True, vmem_limit_bytes=VMEM_LIMIT),
        name="poisson_gradient",
    )(
        activity.reshape(area, width), histo_counts, background,
        jnp.swapaxes(blur_values, 2, 3).reshape(total, band, width), jnp.swapaxes(band_start, 0, 1),
    )


def solution(mesh):
    placed = (
        P(("parts", "view"), "slab", None),
        P(("parts", "view"), None, "slab", None),
        P(("parts", "view"), "slab", None),
        P("view", None, None, None),
        P("view", None, None),
    )
    return jax.shard_map(
        per_device,
        mesh=mesh,
        in_specs=placed,
        out_specs=P(("parts", "view"), "slab", None),
        check_vma=False,
    )
```

time: 24.7 us -> 22.7 us (0.919)
  the two profiles are of different devices: /device:TPU:0 before, /device:TPU:31 now
where the time goes in v3:
time: 22.7 us; the launch traced here: 22.6 us
  Pallas kernels  21.9 us (96%)
  local copies, waits for them, and re-layouts  0.66 us (3%)
    pallas_call x1, Pallas kernels, per_device(): pl.pallas_call(functools.partial(kernel, groups), out_shape=pltpu.VMEM(bl...  21.9 us
    unnamed x1, local copies, waits for them, and re-layouts  0.66 us

profile of v3, /device:TPU:31, one launch (start us, length us, event | category | flops | bytes accessed | tf_op | source)
XLA Modules:
  0.0 22.6 jit_solution(4147573252709822940)
XLA Ops:
  0.0 21.9 %poisson_gradient.1 = f32[8,16,256]{2,1,0:T(8,128)S(1)} custom-call(bf16[128,256]{1,0:T(8,128)(2,1)} %bitcast.6, s32[2,64,16,256]{3,2,1,0:T(8,128)} %counts_hbm.1, bf16[2,16,256]{2,1,0:T(8,128)(2,1)} %back_hbm.1, bf16[6,32,256]{2,1,0:T(8,128)(2,1)} %bitcast.5, s32[3,2,256]{2,1,0:T(2,128)} %bitcast.7), custom_call_target="tpu_custom_call" | custom-call | tf_op jit(solution)/shard_map/poisson_gradient/pallas_call | solution.py:367
  21.9 0.7 %copy.7 = f32[8,16,256]{2,1,0:T(8,128)} copy(f32[8,16,256]{2,1,0:T(8,128)S(1)} %poisson_gradient.1) | data formatting | bytes 262144

commit v4 on v3

--- a/solution.py
+++ b/solution.py
@@ -48,13 +48,18 @@
     views = back_hbm.shape[0]
     total = values_hbm.shape[0]
     taps = total // views
-    half = total // 2
 
     def at(hi_index, lo_index, slab_index):
         return (part, hi_index * PAIR + lo_index, slab_index)
 
     def group_at(place):
-        return jnp.where(place == last, hi, jnp.where(place < hi, place, place + 1))
+        rank = last - place
+        both = jnp.minimum(hi, last - hi)
+        inward = jnp.where(hi < last - hi, 1, -1)
+        reach = (rank + 1) // 2
+        around = jnp.where(rank % 2 == 1, hi + inward * reach, hi - inward * reach)
+        beyond = jnp.where(hi < last - hi, rank, place)
+        return jnp.where(rank <= 2 * both, around, beyond)
 
     barrier = pltpu.get_barrier_semaphore()
     pl.semaphore_signal(barrier, inc=1, device_id=at(hi, lo, 1 - slab), device_id_type=MESH)
@@ -98,6 +103,7 @@
 
     pl.semaphore_wait(barrier, 1 + hi + lo)
 
+
     @pl.when(lo == 1)
     def _():
         pl.semaphore_signal(pair_ready, inc=1, device_id=at(hi, 0, slab), device_id_type=MESH)
@@ -132,17 +138,26 @@
             device_id=at(hi, lo, 1 - slab), device_id_type=MESH,
         )
 
-    landed = values_ref.at[pl.ds(total + slab * half, half)]
-    swaps = [
+    bands = [
         to_pair(source, target, swap_send.at[index], swap_recv.at[index])
         for index, (source, target) in enumerate(
-            (
-                (values_hbm.at[pl.ds(slab * half, half)], landed),
-                (starts_hbm, starts_ref.at[1]), (back_hbm, back_ref.at[1]),
-            )
+            ((values_hbm, values_ref.at[pl.ds(total, total)]), (starts_hbm, starts_ref.at[1]))
         )
     ]
-    share = to_core(landed, landed, share_send, share_recv)
+    shares = [
+        to_core(target, target, share_send.at[index], share_recv.at[index])
+        for index, target in enumerate((values_ref.at[pl.ds(total, total)], starts_ref.at[1]))
+    ]
+    level_copy = to_pair(back_hbm, back_ref.at[1], swap_send.at[2], swap_recv.at[2])
+
+    def start_swaps():
+        @pl.when(slab == 1)
+        def _():
+            for copy in bands:
+                copy.start()
+
+        level_copy.start()
+
     edge_copy = to_core(edge_own, edge_of(hi), edge_send, edge_recv)
 
     def trade(place):
@@ -165,8 +180,7 @@
 
     @pl.when(lo == 1)
     def _():
-        for copy in swaps:
-            copy.start()
+        start_swaps()
 
     loads[0].wait()
     for target in range(last):
@@ -187,8 +201,7 @@
     @pl.when(lo == 0)
     def _():
         pl.semaphore_wait(pair_ready, 1)
-        for copy in swaps:
-            copy.start()
+        start_swaps()
 
     send_counts(0)
 
@@ -250,10 +263,19 @@
             block_copy(target).start()
             rim_copy(target).start()
 
-    for copy in swaps:
-        copy.wait_recv()
-    share.start()
-    share.wait_recv()
+
+    @pl.when(slab == 1)
+    def _():
+        for index in range(2):
+            bands[index].wait_recv()
+            shares[index].start()
+
+    @pl.when(slab == 0)
+    def _():
+        for copy in shares:
+            copy.wait_recv()
+
+    level_copy.wait_recv()
     for which in range(total):
         build(which, 1)
 
@@ -282,6 +304,26 @@
             [x.reshape(-1, width).astype(jnp.bfloat16) for x in (lower, image, upper)], axis=1
         )
         summed[...] = jnp.dot(stacked, forward_w[...], preferred_element_type=jnp.float32)
+
+        @pl.when((place == last) & (slab == 1))
+        def _():
+            for copy in bands + shares:
+                copy.wait_send()
+
+        @pl.when(place == last)
+        def _():
+            level_copy.wait_send()
+            edge_copy.wait_send()
+            for done in range(last):
+                target = group_at(done)
+                halo_copy(done).wait_send()
+                trade(done).wait_send()
+                block_copy(target).wait_send()
+                rim_copy(target).wait_send()
+                if done < last - 1:
+                    for copy in sum_copies(target):
+                        copy.wait_send()
+
 
         def ratios_of(slot, events):
             ratios = []
@@ -338,19 +380,10 @@
         whole[...] += decode(owner_code[source], owner_unit[source])
     out_ref[...] = whole[...]
 
-    for copy in swaps:
+    halo_copy(last).wait_send()
+    trade(last).wait_send()
+    for copy in sum_copies(group_at(last - 1)):
         copy.wait_send()
-    share.wait_send()
-    edge_copy.wait_send()
-    for place in range(groups):
-        halo_copy(place).wait_send()
-        trade(place).wait_send()
-    for place in range(last):
-        target = group_at(place)
-        block_copy(target).wait_send()
-        rim_copy(target).wait_send()
-        for copy in sum_copies(target):
-            copy.wait_send()
 
 
 def per_device(activity, histo_counts, background, blur_values, band_start):
@@ -395,7 +428,7 @@
             pltpu.SemaphoreType.REGULAR((groups,)),
             pltpu.SemaphoreType.REGULAR,
             dma((groups,)), dma((groups,)), dma((groups,)), dma((groups,)),
-            dma((3,)), dma((3,)), dma, dma, dma((groups,)), dma((groups,)),
+            dma((3,)), dma((3,)), dma((2,)), dma((2,)), dma((groups,)), dma((groups,)),
             dma, dma, dma((groups,)), dma((groups,)),
             dma((groups,)), dma((groups,)), dma((groups,)), dma((groups,)),
         ],

time: 22.7 us -> 20 us (0.88)
  the two profiles are of different devices: /device:TPU:31 before, /device:TPU:0 now
where the time goes in v4:
time: 20 us; the launch traced here: 19.9 us
  Pallas kernels  19.2 us (96%)
  local copies, waits for them, and re-layouts  0.66 us (3%)
    pallas_call x1, Pallas kernels, per_device(): pl.pallas_call(functools.partial(kernel, groups), out_shape=pltpu.VMEM(bl...  19.2 us
    unnamed x1, local copies, waits for them, and re-layouts  0.66 us

profile of v4, /device:TPU:0, one launch (start us, length us, event | category | flops | bytes accessed | tf_op | source)
XLA Modules:
  0.0 19.9 jit_solution(13334647124405071104)
XLA Ops:
  0.0 19.2 %poisson_gradient.1 = f32[8,16,256]{2,1,0:T(8,128)S(1)} custom-call(bf16[128,256]{1,0:T(8,128)(2,1)} %bitcast.6, s32[2,64,16,256]{3,2,1,0:T(8,128)} %counts_hbm.1, bf16[2,16,256]{2,1,0:T(8,128)(2,1)} %back_hbm.1, bf16[6,32,256]{2,1,0:T(8,128)(2,1)} %bitcast.5, s32[3,2,256]{2,1,0:T(2,128)} %bitcast.7), custom_call_target="tpu_custom_call" | custom-call | tf_op jit(solution)/shard_map/poisson_gradient/pallas_call | solution.py:400
  19.2 0.7 %copy.7 = f32[8,16,256]{2,1,0:T(8,128)} copy(f32[8,16,256]{2,1,0:T(8,128)S(1)} %poisson_gradient.1) | data formatting | bytes 262144
